TPU v7x, 32 devices: a whole 2x2x4 slice. The times are simulated.
32 devices in a mesh: fsdp: 4 (over y, x), ctx: 4 (over z), tp: 2 (over core).
Axes of the slice: x: 2, y: 2, z: 4, core: 2. Of those that a mesh axis runs over, the one named last changes fastest.
Arguments:
- tokens: bfloat16 [4, 2048, 1024], P('fsdp', 'ctx'), may hold values from -6 to 6
- segment_ids: int32 [4, 2048], P('fsdp', 'ctx'), may hold values from 0 to 10, as said below
- positions: int32 [4, 2048], P('fsdp', 'ctx'), may hold values from 0 to 2047, as said below
- attention_gain: bfloat16 [1024], P('fsdp'), may hold values from 0.099609375 to 1.8984375
- attention_shift: bfloat16 [1024], P('fsdp'), may hold values from -1.75 to 1.75
- feedforward_gain: bfloat16 [1024], P('fsdp'), may hold values from 0.099609375 to 1.8984375
- feedforward_shift: bfloat16 [1024], P('fsdp'), may hold values from -1.75 to 1.75
- joint_weight: bfloat16 [1024, 3, 1024], P('fsdp', None, 'tp'), may hold values from -8 to 8
- joint_bias: bfloat16 [3, 1024], P(None, ('tp', 'fsdp')), may hold values from -3 to 3
- output_weight: bfloat16 [1024, 1024], P('tp', 'fsdp'), may hold values from -1.5 to 1.5
- output_bias: bfloat16 [1024], P('fsdp'), may hold values from -1.75 to 1.75
- up_weight: bfloat16 [1024, 4096], P('fsdp', 'tp'), may hold values from -0.1875 to 0.1875
- up_bias: bfloat16 [4096], P(('tp', 'fsdp')), may hold values from -3 to 3
- down_weight: bfloat16 [4096, 1024], P('tp', 'fsdp'), may hold values from -0.09375 to 0.09375
- down_bias: bfloat16 [1024], P('fsdp'), may hold values from -1.75 to 1.75
- cotangent: float32 [4, 2048, 1024], P('fsdp', 'ctx'), may hold values from -6 to 6
Outputs:
- result: float32 [4, 2048, 1024], P('fsdp', 'ctx')
- tokens_grad: float32 [4, 2048, 1024], P('fsdp', 'ctx')
- attention_gain_grad: float32 [1024], P('fsdp')
- attention_shift_grad: float32 [1024], P('fsdp')
- feedforward_gain_grad: float32 [1024], P('fsdp')
- feedforward_shift_grad: float32 [1024], P('fsdp')
- joint_weight_grad: float32 [1024, 3, 1024], P('fsdp', None, 'tp')
- joint_bias_grad: float32 [3, 1024], P(None, ('tp', 'fsdp'))
- output_weight_grad: float32 [1024, 1024], P('tp', 'fsdp')
- output_bias_grad: float32 [1024], P('fsdp')
- up_weight_grad: float32 [1024, 4096], P('fsdp', 'tp')
- up_bias_grad: float32 [4096], P(('tp', 'fsdp'))
- down_weight_grad: float32 [4096, 1024], P('tp', 'fsdp')
- down_bias_grad: float32 [1024], P('fsdp')
Inputs may be any that keep to these rules, and one draw needn't show every extreme that they name: `segment_ids`: along each sequence the ids start at 0 and rise by one at each document's first token; a document holds 204 to 2048 tokens, the last one cut at the sequence's end. The first sequence is one document; the last sequence is documents of 204 tokens. `positions`: each token's offset from the first token of its document; the first sequence is one document.
All inputs are finite; a program needn't handle non-finite values.
Results may differ from a plain program's by a relative error of at most 0.011.
Values may be sent and summed in bfloat16 or wider, within the bound.
No kernel may reach another device: no remote copies, remote signals or barrier semaphores. Data moves between devices by JAX's collectives and lax.ppermute only.
A program may use at most 192 MiB of HBM per device.

v0:
```python
import jax
import jax.numpy as jnp
from jax import lax
from jax.sharding import PartitionSpec as P

HD = 64
ROT = 16
EPS = 1e-05
ROPE_BASE = 10000.0


def rope_tables(offsets):
    half_dim = ROT // 2
    freq = ROPE_BASE ** (-(jnp.arange(half_dim, dtype=jnp.float32) * 2.0 / ROT))
    angle = offsets.astype(jnp.float32)[:, None] * freq[None, :]
    return (jnp.cos(angle)[:, None, :], jnp.sin(angle)[:, None, :])


def rotate(tensor, cosine, sine):
    half_dim = ROT // 2
    front = tensor[..., :half_dim]
    middle = tensor[..., half_dim:ROT]
    return jnp.concatenate(
        [front * cosine - middle * sine, middle * cosine + front * sine, tensor[..., ROT:]], axis=-1
    )


def unrotate(grads, cosine, sine):
    half_dim = ROT // 2
    front = grads[..., :half_dim]
    middle = grads[..., half_dim:ROT]
    return jnp.concatenate(
        [front * cosine + middle * sine, middle * cosine - front * sine, grads[..., ROT:]], axis=-1
    )


def normalize(rows):
    center = jnp.mean(rows, -1, keepdims=True)
    centred = rows - center
    spread = jnp.mean(centred * centred, -1, keepdims=True)
    rstd = lax.rsqrt(spread + EPS)
    return (centred * rstd, rstd)


def norm_back(upstream, normed, rstd, gain):
    scaled = upstream * gain
    return rstd * (
        scaled
        - jnp.mean(scaled, -1, keepdims=True)
        - normed * jnp.mean(scaled * normed, -1, keepdims=True)
    )


def masked_scores(query_blk, query_index, query_seg, keys, key_seg):
    scores = jnp.einsum(
        "qhe,khe->hqk", query_blk, keys, preferred_element_type=jnp.float32
    ) * HD ** (-0.5)
    key_index = jnp.arange(keys.shape[0], dtype=jnp.int32)
    allowed = (key_seg[None, :] == query_seg[:, None]) & (
        key_index[None, :] <= query_index[:, None]
    )
    return jnp.where(allowed[None], scores, -jnp.inf)


def local(
    tokens,
    segment_ids,
    positions,
    attention_gain,
    attention_shift,
    feedforward_gain,
    feedforward_shift,
    joint_weight,
    joint_bias,
    output_weight,
    output_bias,
    up_weight,
    up_bias,
    down_weight,
    down_bias,
    cotangent,
):
    f32 = jnp.float32
    bf16 = jnp.bfloat16
    scale = HD ** (-0.5)
    small = jnp.stack(
        [
            attention_gain,
            attention_shift,
            feedforward_gain,
            feedforward_shift,
            output_bias,
            down_bias,
        ]
    )
    full_joint, full_output, full_up, full_down, full_small, full_jbias, full_upbias = (
        lax.all_gather(joint_weight, "fsdp", axis=0, tiled=True),
        lax.all_gather(output_weight, "fsdp", axis=1, tiled=True),
        lax.all_gather(up_weight, "fsdp", axis=0, tiled=True),
        lax.all_gather(down_weight, "fsdp", axis=1, tiled=True),
        lax.all_gather(small, "fsdp", axis=1, tiled=True),
        lax.all_gather(joint_bias, "fsdp", axis=1, tiled=True),
        lax.all_gather(up_bias, "fsdp", axis=0, tiled=True),
    )
    params = full_small.astype(f32)
    gain_one = params[0]
    shift_one = params[1]
    gain_two = params[2]
    shift_two = params[3]
    rows = tokens[0].astype(f32)
    count_rows = rows.shape[0]
    local_width = joint_weight.shape[2]
    heads_here = local_width // HD
    normed, rstd = normalize(rows)
    first = (normed * gain_one + shift_one).astype(bf16)
    second = (normed * gain_two + shift_two).astype(bf16)
    joint = (
        jnp.einsum("nd,dpe->npe", first, full_joint, preferred_element_type=f32)
        + full_jbias.astype(f32)[None]
    )
    cosine, sine = rope_tables(positions[0])
    queries = rotate(joint[:, 0].reshape(count_rows, heads_here, HD), cosine, sine).astype(bf16)
    keys_here = rotate(joint[:, 1].reshape(count_rows, heads_here, HD), cosine, sine).astype(bf16)
    values_here = joint[:, 2].reshape(count_rows, heads_here, HD).astype(bf16)
    seg_here = segment_ids[0]
    all_keys, all_values, all_segs = (
        lax.all_gather(keys_here, "ctx", axis=0, tiled=True),
        lax.all_gather(values_here, "ctx", axis=0, tiled=True),
        lax.all_gather(seg_here.astype(bf16), "ctx", axis=0, tiled=True),
    )
    key_seg = all_segs.astype(f32)
    query_seg = seg_here.astype(f32)
    query_index = lax.axis_index("ctx") * count_rows + jnp.arange(count_rows, dtype=jnp.int32)
    block = min(512, count_rows)
    count_blocks = count_rows // block
    query_blocks = queries.reshape(count_blocks, block, heads_here, HD)
    index_blocks = query_index.reshape(count_blocks, block)
    seg_blocks = query_seg.reshape(count_blocks, block)

    def forward_block(args):
        query_blk, block_index, block_seg = args
        scores = masked_scores(query_blk, block_index, block_seg, all_keys, key_seg)
        top = jnp.max(scores, -1, keepdims=True)
        lse = top + jnp.log(jnp.sum(jnp.exp(scores - top), -1, keepdims=True))
        probs = jnp.exp(scores - lse).astype(bf16)
        mixed = jnp.einsum("hqk,khe->qhe", probs, all_values, preferred_element_type=f32)
        return (mixed, lse[..., 0])

    context32, lse_all = lax.map(forward_block, (query_blocks, index_blocks, seg_blocks))
    context32 = context32.reshape(count_rows, local_width)
    context = context32.astype(bf16)
    upper = jnp.dot(second, full_up, preferred_element_type=f32) + full_upbias.astype(f32)
    activated = jax.nn.gelu(upper, approximate=False).astype(bf16)
    partial_value = jnp.dot(context, full_output, preferred_element_type=f32) + jnp.dot(
        activated, full_down, preferred_element_type=f32
    )
    mixed_all = lax.psum(partial_value, "tp")
    result = rows + mixed_all + params[4] + params[5]
    back_joint, back_output, back_up, back_down = (
        lax.all_gather(joint_weight, "fsdp", axis=0, tiled=True),
        lax.all_gather(output_weight, "fsdp", axis=1, tiled=True),
        lax.all_gather(up_weight, "fsdp", axis=0, tiled=True),
        lax.all_gather(down_weight, "fsdp", axis=1, tiled=True),
    )
    cot = cotangent[0]
    cot_b = cot.astype(bf16)
    grad_output_w = jnp.dot(context.T, cot_b, preferred_element_type=f32)
    bias_sum = jnp.sum(cot, 0)
    grad_down_w = jnp.dot(activated.T, cot_b, preferred_element_type=f32)
    d_act = jnp.einsum("nd,fd->nf", cot_b, back_down, preferred_element_type=f32)
    unused, gelu_back = jax.vjp(lambda value: jax.nn.gelu(value, approximate=False), upper)
    d_upper = gelu_back(d_act)[0]
    d_upper_b = d_upper.astype(bf16)
    grad_up_w = jnp.dot(second.T, d_upper_b, preferred_element_type=f32)
    grad_up_b = jnp.sum(d_upper, 0)
    d_second_part = jnp.einsum("nf,df->nd", d_upper_b, back_up, preferred_element_type=f32)
    d_context = (
        jnp.einsum("nd,wd->nw", cot_b, back_output, preferred_element_type=f32)
        .astype(bf16)
        .reshape(count_rows, heads_here, HD)
    )
    delta = jnp.sum(d_context.astype(f32) * context32.reshape(count_rows, heads_here, HD), -1)
    dctx_blocks = d_context.reshape(count_blocks, block, heads_here, HD)

    def backward_block(args):
        query_blk, block_index, block_seg, dctx_blk, delta_blk, lse_blk = args
        scores = masked_scores(query_blk, block_index, block_seg, all_keys, key_seg)
        probs = jnp.exp(scores - lse_blk[..., None]).astype(bf16)
        d_probs = jnp.einsum("qhe,khe->hqk", dctx_blk, all_values, preferred_element_type=f32)
        d_scores = (probs.astype(f32) * (d_probs - jnp.transpose(delta_blk)[..., None])).astype(
            bf16
        )
        d_query_blk = (
            jnp.einsum("hqk,khe->qhe", d_scores, all_keys, preferred_element_type=f32) * scale
        )
        return (probs, d_scores, d_query_blk)

    probs_all, dscores_all, d_queries = lax.map(
        backward_block,
        (
            query_blocks,
            index_blocks,
            seg_blocks,
            dctx_blocks,
            delta.reshape(count_blocks, block, heads_here),
            lse_all,
        ),
    )
    d_queries = d_queries.reshape(count_rows, heads_here, HD)
    key_part = (
        jnp.einsum("bhqk,bqhe->khe", dscores_all, query_blocks, preferred_element_type=f32) * scale
    )
    value_part = jnp.einsum("bhqk,bqhe->khe", probs_all, dctx_blocks, preferred_element_type=f32)
    key_value = lax.psum_scatter(
        jnp.concatenate(
            [
                key_part.reshape(count_rows * lax.axis_size("ctx"), local_width),
                value_part.reshape(count_rows * lax.axis_size("ctx"), local_width),
            ],
            axis=1,
        ),
        "ctx",
        scatter_dimension=0,
        tiled=True,
    )
    d_keys = key_value[:, :local_width].reshape(count_rows, heads_here, HD)
    d_values = key_value[:, local_width:]
    d_joint = jnp.stack(
        [
            unrotate(d_queries, cosine, sine).reshape(count_rows, local_width),
            unrotate(d_keys, cosine, sine).reshape(count_rows, local_width),
            d_values,
        ],
        axis=1,
    )
    d_joint_b = d_joint.astype(bf16)
    grad_joint_w = jnp.einsum("nd,npe->dpe", first, d_joint_b, preferred_element_type=f32)
    grad_joint_b = jnp.sum(d_joint, 0)
    d_first_part = jnp.einsum("npe,dpe->nd", d_joint_b, back_joint, preferred_element_type=f32)
    d_first, d_second = lax.psum((d_first_part, d_second_part), "tp")
    norm_stats = jnp.stack(
        [
            jnp.sum(d_first * normed, 0),
            jnp.sum(d_first, 0),
            jnp.sum(d_second * normed, 0),
            jnp.sum(d_second, 0),
        ]
    )
    tokens_grad = (
        cot
        + norm_back(d_first, normed, rstd, gain_one)
        + norm_back(d_second, normed, rstd, gain_two)
    )
    grad_small = jnp.concatenate([norm_stats, bias_sum[None], bias_sum[None]], axis=0)
    share_joint, share_output, share_up, share_down, share_small, share_jbias, share_upbias = (
        lax.psum_scatter(grad_joint_w, ("fsdp", "ctx"), scatter_dimension=0, tiled=True),
        lax.psum_scatter(grad_output_w, ("fsdp", "ctx"), scatter_dimension=1, tiled=True),
        lax.psum_scatter(grad_up_w, ("fsdp", "ctx"), scatter_dimension=0, tiled=True),
        lax.psum_scatter(grad_down_w, ("fsdp", "ctx"), scatter_dimension=1, tiled=True),
        lax.psum_scatter(grad_small, ("fsdp", "ctx"), scatter_dimension=1, tiled=True),
        lax.psum_scatter(grad_joint_b, ("fsdp", "ctx"), scatter_dimension=1, tiled=True),
        lax.psum_scatter(grad_up_b, ("fsdp", "ctx"), scatter_dimension=0, tiled=True),
    )
    owned = (
        lax.all_gather(share_joint, "ctx", axis=0, tiled=True),
        lax.all_gather(share_output, "ctx", axis=1, tiled=True),
        lax.all_gather(share_up, "ctx", axis=0, tiled=True),
        lax.all_gather(share_down, "ctx", axis=1, tiled=True),
        lax.all_gather(share_small, "ctx", axis=1, tiled=True),
        lax.all_gather(share_jbias, "ctx", axis=1, tiled=True),
        lax.all_gather(share_upbias, "ctx", axis=0, tiled=True),
    )
    owned_joint, owned_output, owned_up, owned_down, owned_small, owned_jbias, owned_upbias = owned
    return (
        result[None],
        tokens_grad[None],
        owned_small[0],
        owned_small[1],
        owned_small[2],
        owned_small[3],
        owned_joint,
        owned_jbias,
        owned_output,
        owned_small[4],
        owned_up,
        owned_upbias,
        owned_down,
        owned_small[5],
    )


def solution(mesh):
    placed = (
        P("fsdp", "ctx", None),
        P("fsdp", "ctx"),
        P("fsdp", "ctx"),
        P("fsdp"),
        P("fsdp"),
        P("fsdp"),
        P("fsdp"),
        P("fsdp", None, "tp"),
        P(None, ("tp", "fsdp")),
        P("tp", "fsdp"),
        P("fsdp"),
        P("fsdp", "tp"),
        P(("tp", "fsdp")),
        P("tp", "fsdp"),
        P("fsdp"),
        P("fsdp", "ctx", None),
    )
    return jax.shard_map(
        local,
        mesh=mesh,
        in_specs=placed,
        out_specs=(
            P("fsdp", "ctx", None),
            P("fsdp", "ctx", None),
            P("fsdp"),
            P("fsdp"),
            P("fsdp"),
            P("fsdp"),
            P("fsdp", None, "tp"),
            P(None, ("tp", "fsdp")),
            P("tp", "fsdp"),
            P("fsdp"),
            P("fsdp", "tp"),
            P(("tp", "fsdp")),
            P("tp", "fsdp"),
            P("fsdp"),
        ),
        check_vma=False,
    )
```

profile of v0, /device:TPU:0, one launch (start us, length us, event | category | flops | bytes accessed | tf_op | source)
XLA Modules:
  0.0 1352.6 jit_solution(17469226401049093940)
XLA Ops:
  31.2 26.0 %all-gather.15.cloned.1.call-done = bf16[1024,3,512]{0,2,1:T(8,128)(2,1)} async-done(((bf16[256,3,512]{0,2,1:T(8,128)(2,1)}), bf16[1024,3,512]{0,2,1:T(8,128)(2,1)}) %all-gather.15.cloned.1.call-update) | async-done | bytes 3145744 | tf_op jit(solution)/shard_map/all_gather | solution.py:97
  67.5 11.9 all-gather
  89.5 44.2 %all-gather.19.cloned.1.call-done = bf16[2048,8,64]{0,2,1:T(8,128)(2,1)} async-done(((bf16[512,8,64]{0,2,1:T(8,128)(2,1)}), bf16[2048,8,64]{0,2,1:T(8,128)(2,1)}) %all-gather.19.cloned.1.call-update) | async-done | bytes 2097168 | tf_op jit(solution)/shard_map/all_gather | solution.py:127
  133.6 16.0 %fusion = (f32[8,512]{1,0:T(8,128)S(1)}, f32[8,512,2048]{2,1,0:T(8,128)}) fusion(pred[512,2048]{1,0:T(8,128)(4,1)S(1)} %fusion.7, bf16[2048,8,64]{0,2,1:T(8,128)(2,1)} %all-gather.19.cloned.1.call-done, bf16[512,8,48]{0,2,1:T(8,128)(2,1)S(1)} %slice.170, bf16[512,8,8]{0,2,1:T(8,128)(2,1)} %get-tuple-element.148, bf16[512,8,8]{0,2,1:T(8,128)(2,1)} %get-tuple-element.147), kind=kOutput, calls=%fused_computation.4 | convolution fusion | flops 1100476416 | bytes 37240832 | tf_op jit(solution)/shard_map/while/body/eval_jaxpr/qhe,khe->hqk/dot_general | solution.py:55
  149.6 15.9 %exponential_reduce_fusion = f32[8,512]{1,0:T(8,128)S(1)} fusion(f32[8,512,2048]{2,1,0:T(8,128)} %get-tuple-element.176, f32[8,512]{1,0:T(8,128)S(1)} %get-tuple-element.175, pred[512,2048]{1,0:T(8,128)(4,1)S(1)} %fusion.7), kind=kLoop, calls=%fused_computation.2 | loop fusion | flops 33550336 | bytes 34635776 | tf_op jit(solution)/shard_map/while/body/eval_jaxpr/reduce_sum | solution.py:144
  180.3 12.4 multiply_reduce_fusion.2
  192.7 25.3 %multiply_convert_fusion = bf16[8,512,2048]{2,1,0:T(8,128)(2,1)} fusion(bf16[8,512,2048]{2,1,0:T(8,128)(2,1)} %exponential_convert_fusion, bf16[512,8,64]{0,2,1:T(8,128)(2,1)S(1)} %bitcast.212, bf16[2048,8,64]{0,2,1:T(8,128)(2,1)} %all-gather.17.cloned.1.call-done, f32[8,512]{1,0:T(8,128)S(1)} %bitcast.227), kind=kOutput, calls=%fused_computation | convolution fusion | flops 1107296256 | bytes 36192256 | tf_op jit(solution)/shard_map/while/body/eval_jaxpr/qhe,khe->hqk/dot_general | solution.py:189
  267.5 15.1 %multiply_convert_fusion.1 = (bf16[512,2048]{1,0:T(8,128)(2,1)}, f32[512,2048]{1,0:T(8,128)}, f32[512,2048]{1,0:T(8,128)}) fusion(f32[2048]{0:T(1024)S(1)} %bitcast.253, bf16[1024,2048]{1,0:T(8,128)(2,1)} %all-gather.23.cloned.1.call-done, bf16[1,512,1024]{2,1,0:T(8,128)(2,1)S(1)} %copy-done.3, f32[1024]{0:T(1024)S(1)} %bitcast.257, f32[1024]{0:T(1024)S(1)} %bitcast.234, ...), kind=kOutput, calls=%fused_computation.9 | convolution fusion | flops 2219835392 | bytes 15749120 | tf_op jit(solution)/shard_map/dot_general | solution.py:152
  320.6 12.7 fusion.41
  339.6 95.1 %reduce-scatter.12.cloned.1.call-done = f32[512,1024]{1,0:T(8,128)} async-done(((f32[2048,1024]{1,0:T(8,128)}), f32[512,1024]{1,0:T(8,128)}) %reduce-scatter.12.cloned.1.call-update) | async-done | bytes 2097168 | tf_op jit(solution)/shard_map/reduce_scatter | solution.py:214
  470.1 149.9 %reduce-scatter.18.cloned.1.call-done = f32[64,2048]{1,0:T(8,128)} async-done(((f32[1024,2048]{1,0:T(8,128)}), f32[64,2048]{1,0:T(8,128)}) %reduce-scatter.18.cloned.1.call-update) | async-done | bytes 524304 | tf_op jit(solution)/shard_map/reduce_scatter | solution.py:258
  620.1 182.1 %reduce-scatter.20.cloned.1.call-done = f32[2048,64]{0,1:T(8,128)} async-done(((f32[2048,1024]{0,1:T(8,128)}), f32[2048,64]{0,1:T(8,128)}) %reduce-scatter.20.cloned.1.call-update) | async-done | bytes 524304 | tf_op jit(solution)/shard_map/reduce_scatter | solution.py:259
  802.4 33.3 %all-reduce.4.cloned.1.call-done = (f32[512,1024]{1,0:T(8,128)}, f32[512,1024]{1,0:T(8,128)}, f32[512,1024]{1,0:T(8,128)}) async-done(((f32[512,1024]{1,0:T(8,128)}, f32[512,1024]{1,0:T(8,128)}, f32[512,1024]{1,0:T(8,128)}), (f32[512,1024]{1,0:T(8,128)}, f32[512,1024]{1,0:T(8,128)}, f32[512,1024]{1,0:T(8,128)})) %all-reduce.4.cloned.1.call-update) | async-done | bytes 6291472 | tf_op jit(solution)/shard_map/psum | solution.py:157
  840.2 137.3 %reduce-scatter.14.cloned.1.call-done = f32[64,3,512]{2,0,1:T(8,128)} async-done(((f32[1024,3,512]{2,0,1:T(8,128)}), f32[64,3,512]{2,0,1:T(8,128)}) %reduce-scatter.14.cloned.1.call-update) | async-done | bytes 393232 | tf_op jit(solution)/shard_map/reduce_scatter | solution.py:256
  978.8 39.4 %all-reduce = f32[2048]{0:T(1024)S(1)} all-reduce(f32[2048]{0:T(1024)S(1)} %get-tuple-element.179), channel_id=9, replica_groups=mesh['fsdp'=4,'ctx'=4,'tp'=2] {'fsdp','ctx'}, use_global_device_ids=true, to_apply=%region_25.26.clone | all-reduce | flops 2048 | bytes 16384
  1026.1 36.4 %reduce-scatter.16.cloned.1.call-done = f32[512,64]{0,1:T(8,128)} async-done(((f32[512,1024]{0,1:T(8,128)}), f32[512,64]{0,1:T(8,128)}) %reduce-scatter.16.cloned.1.call-update) | async-done | bytes 131088 | tf_op jit(solution)/shard_map/reduce_scatter | solution.py:257
  1062.5 15.7 %all_gather.68 = f32[512,256]{0,1:T(8,128)} all-gather(f32[512,64]{0,1:T(8,128)} %reduce-scatter.16.cloned.1.call-done), channel_id=1, replica_groups=mesh['fsdp'=4,'ctx'=4,'tp'=2] {'ctx'}, dimensions={1}, use_global_device_ids=true | all-gather | bytes 655360 | tf_op jit(solution)/shard_map/all_gather | solution.py:266
  1080.2 57.7 %reduce-scatter.24.cloned.1.call-done = f32[32,3]{1,0:T(8,128)} async-done(((f32[512,3]{1,0:T(8,128)}), f32[32,3]{1,0:T(8,128)}) %reduce-scatter.24.cloned.1.call-update) | async-done | bytes 400
  1138.7 12.2 all-gather.3
  1151.6 30.2 %all-gather.29.cloned.1.call-done = f32[256,2048]{1,0:T(8,128)} async-done(((f32[64,2048]{1,0:T(8,128)}), f32[256,2048]{1,0:T(8,128)}) %all-gather.29.cloned.1.call-update) | async-done | bytes 2097168 | tf_op jit(solution)/shard_map/all_gather | solution.py:267
  1181.7 46.1 %all-gather.31.cloned.1.call-done = f32[2048,256]{0,1:T(8,128)} async-done(((f32[2048,64]{0,1:T(8,128)}), f32[2048,256]{0,1:T(8,128)}) %all-gather.31.cloned.1.call-update) | async-done | bytes 2097168 | tf_op jit(solution)/shard_map/all_gather | solution.py:268
  1235.6 70.6 %reduce-scatter.22.cloned.1.call-done = f32[64,6]{1,0:T(8,128)} async-done(((f32[1024,6]{1,0:T(8,128)}), f32[64,6]{1,0:T(8,128)}) %reduce-scatter.22.cloned.1.call-update) | async-done | bytes 1552
  1307.1 13.4 all-gather.2
  1321.1 20.2 %all-gather.27.cloned.1.call-done = f32[256,3,512]{2,0,1:T(8,128)} async-done(((f32[64,3,512]{2,0,1:T(8,128)}), f32[256,3,512]{2,0,1:T(8,128)}) %all-gather.27.cloned.1.call-update) | async-done | bytes 1572880 | tf_op jit(solution)/shard_map/all_gather | solution.py:265
  (190 shorter events, 218.4 us)
Async XLA Ops:
  7.3 49.9 %all-gather.15.cloned.1.call-start = ((), (), s32[]{:S(2)}) async-start(), calls=%async_computation.7 | async-start | bytes 3932160 | tf_op jit(solution)/shard_map/all_gather | solution.py:97
  9.7 75.8 %all-gather.21.cloned.1.call-start = ((), (), s32[]{:S(2)}) async-start(), calls=%async_computation.10 | async-start | bytes 1310720 | tf_op jit(solution)/shard_map/all_gather | solution.py:98
  10.5 123.2 %all-gather.19.cloned.1.call-start = ((), (), s32[]{:S(2)}) async-start(), calls=%async_computation.9 | async-start | bytes 2621440 | tf_op jit(solution)/shard_map/all_gather | solution.py:127
  12.5 48.8 %copy-start.10 = (f32[512,8]{0,1:T(8,128)}, f32[512,8]{0,1:T(8,128)S(1)}, u32[]{:S(2)}) copy-start(f32[512,8]{0,1:T(8,128)S(1)} %get-tuple-element.171) | copy-start | bytes 49156
  64.1 116.3 %all-gather.17.cloned.1.call-start = ((), (), s32[]{:S(2)}) async-start(), calls=%async_computation.8 | async-start | bytes 2621440 | tf_op jit(solution)/shard_map/all_gather | solution.py:128
  66.2 201.3 %all-gather.23.cloned.1.call-start = ((), (), s32[]{:S(2)}) async-start(), calls=%async_computation.11 | async-start | bytes 5242880 | tf_op jit(solution)/shard_map/all_gather | solution.py:99
  66.8 221.0 %all-gather.25.cloned.1.call-start = ((), (), s32[]{:S(2)}) async-start(), calls=%async_computation.12 | async-start | bytes 5242880 | tf_op jit(solution)/shard_map/all_gather | solution.py:100
  67.4 367.3 %reduce-scatter.12.cloned.1.call-start = ((), (), s32[]{:S(2)}) async-start(), calls=%async_computation.13 | async-start | bytes 10485760 | tf_op jit(solution)/shard_map/reduce_scatter | solution.py:214
  258.8 361.2 %reduce-scatter.18.cloned.1.call-start = ((), (), s32[]{:S(2)}) async-start(), calls=%async_computation.17 | async-start | bytes 8912896 | tf_op jit(solution)/shard_map/reduce_scatter | solution.py:258
  302.4 499.7 %reduce-scatter.20.cloned.1.call-start = ((), (), s32[]{:S(2)}) async-start(), calls=%async_computation.19 | async-start | bytes 8912896 | tf_op jit(solution)/shard_map/reduce_scatter | solution.py:259
  309.7 526.0 %all-reduce.4.cloned.1.call-start = ((), (), s32[]{:S(2)}) async-start(), calls=%async_computation.23 | async-start | bytes 12582912 | tf_op jit(solution)/shard_map/psum | solution.py:157
  339.6 101.9 %copy-start.11 = (f32[512,8]{0,1:T(8,128)S(1)}, f32[512,8]{0,1:T(8,128)}, u32[]{:S(2)}) copy-start(f32[512,8]{0,1:T(8,128)} %copy-done.10) | copy-start | bytes 49156
  339.6 101.9 %copy-start.13 = (f32[512,8]{0,1:T(8,128)S(1)}, f32[512,8]{0,1:T(8,128)}, u32[]{:S(2)}) copy-start(f32[512,8]{0,1:T(8,128)} %copy-done.12) | copy-start | bytes 49156
  456.6 520.9 %reduce-scatter.14.cloned.1.call-start = ((), (), s32[]{:S(2)}) async-start(), calls=%async_computation.14 | async-start | bytes 6684672 | tf_op jit(solution)/shard_map/reduce_scatter | solution.py:256
  463.8 598.7 %reduce-scatter.16.cloned.1.call-start = ((), (), s32[]{:S(2)}) async-start(), calls=%async_computation.16 | async-start | bytes 2228224 | tf_op jit(solution)/shard_map/reduce_scatter | solution.py:257
  467.0 670.9 %reduce-scatter.24.cloned.1.call-start = ((), (), s32[]{:S(2)}) async-start(), calls=%async_computation.22 | async-start | bytes 278528
  470.0 711.7 %all-gather.29.cloned.1.call-start = ((), (), s32[]{:S(2)}) async-start(), calls=%async_computation.18 | async-start | bytes 2621440 | tf_op jit(solution)/shard_map/all_gather | solution.py:267
  620.0 607.8 %all-gather.31.cloned.1.call-start = ((), (), s32[]{:S(2)}) async-start(), calls=%async_computation.20 | async-start | bytes 2621440 | tf_op jit(solution)/shard_map/all_gather | solution.py:268
  802.2 175.4 %copy-start.31 = (u32[32]{0:T(128)S(1)}, u32[32]{0:T(128)}, u32[]{:S(2)}) copy-start(u32[32]{0:T(128)} %constant.141) | copy-start | bytes 388
  802.2 504.0 %reduce-scatter.22.cloned.1.call-start = ((), (), s32[]{:S(2)}) async-start(), calls=%async_computation.21 | async-start | bytes 557056
  839.1 391.6 %copy-start.16 = (f32[1,1024]{1,0:T(1,128)S(1)}, f32[1,1024]{1,0:T(1,128)}, u32[]{:S(2)}) copy-start(f32[1,1024]{1,0:T(1,128)} %get-tuple-element.159) | copy-start | bytes 12292
  839.1 391.6 %copy-start.17 = (f32[1,1024]{1,0:T(1,128)S(1)}, f32[1,1024]{1,0:T(1,128)}, u32[]{:S(2)}) copy-start(f32[1,1024]{1,0:T(1,128)} %get-tuple-element.160) | copy-start | bytes 12292
  840.2 501.1 %all-gather.27.cloned.1.call-start = ((), (), s32[]{:S(2)}) async-start(), calls=%async_computation.15 | async-start | bytes 1966080 | tf_op jit(solution)/shard_map/all_gather | solution.py:265
  1235.6 108.4 %copy-start.7 = (f32[256,2048]{1,0:T(8,128)S(1)}, f32[256,2048]{1,0:T(8,128)}, u32[]{:S(2)}) copy-start(f32[256,2048]{1,0:T(8,128)} %all-gather.29.cloned.1.call-done) | copy-start | bytes 6291460
  (27 other events, 299.9 us)
Sparse Core Ops, SparseCore 0:
  10.5 46.6 all-gather.14
  59.0 26.4 all-gather.20
  87.7 45.9 all-gather.18
  135.6 44.6 all-gather.16
  182.0 51.4 all-gather.22
  235.2 52.6 all-gather.24
  290.2 144.4 reduce-scatter.11
  436.9 183.0 reduce-scatter.17
  622.3 179.8 reduce-scatter.19
  805.9 29.7 all-reduce.3
  838.1 139.3 reduce-scatter.13
  980.3 82.1 reduce-scatter.15
  1064.8 73.0 reduce-scatter.23
  1139.3 42.3 all-gather.28
  1183.1 44.6 all-gather.30
  1230.5 75.7 reduce-scatter.21
  1307.7 33.5 all-gather.26
where the time goes:
time: 1360 us; the launch traced here: 1350 us
  waiting for transfers between devices  942 us (69%)
  matrix products  161 us (12%)
  blocking collectives  126 us (9%)
  local copies, waits for them, and re-layouts  54.5 us (4%)
  other arithmetic  52.6 us (4%)
  between operations  15.4 us (1%)
    reduce_scatter x1, waiting for transfers between devices, local(): lax.psum_scatter(grad_down_w, ('fsdp', 'ctx'), scatter_dimension=1, tiled...  182 us
    reduce_scatter x1, waiting for transfers between devices, local(): lax.psum_scatter(grad_up_w, ('fsdp', 'ctx'), scatter_dimension=0, tiled=T...  150 us
    reduce_scatter x1, waiting for transfers between devices, local(): lax.psum_scatter(grad_joint_w, ('fsdp', 'ctx'), scatter_dimension=0, tile...  137 us
    unnamed x19, waiting for transfers between devices  130 us
    reduce_scatter x1, waiting for transfers between devices, local(): lax.psum_scatter(jnp.concatenate([key_part.reshape(count_rows * lax.axis_...  95.1 us
    all_gather x1, waiting for transfers between devices, local(): lax.all_gather(share_down, 'ctx', axis=1, tiled=True)  46.1 us
    all_gather x1, waiting for transfers between devices, local(): lax.all_gather(keys_here, 'ctx', axis=0, tiled=True)  44.2 us
    unnamed x1, blocking collectives  39.4 us
  transfers between devices with their start and end apart: 17, of which 16 were waited for; matrix products, arithmetic and copies ran while one was open for 19% of the time, Pallas kernels for 0%

commit v1 on v0

--- a/solution.py
+++ b/solution.py
@@ -7,6 +7,19 @@
 ROT = 16
 EPS = 1e-05
 ROPE_BASE = 10000.0
+
+
+def gather_around(shard, axis, dim):
+    size, position, extent = (lax.axis_size(axis), lax.axis_index(axis), shard.shape[dim])
+    right = [(i, (i + 1) % size) for i in range(size)]
+    filled = jnp.zeros((*shard.shape[:dim], size * extent, *shard.shape[dim + 1 :]), shard.dtype)
+    current = shard
+    for step in range(size):
+        holder = (position - step) % size
+        filled = lax.dynamic_update_slice_in_dim(filled, current, holder * extent, axis=dim)
+        if step < size - 1:
+            current = lax.ppermute(current, axis, right)
+    return filled
 
 
 def rope_tables(offsets):
@@ -265,7 +278,7 @@
         lax.all_gather(share_joint, "ctx", axis=0, tiled=True),
         lax.all_gather(share_output, "ctx", axis=1, tiled=True),
         lax.all_gather(share_up, "ctx", axis=0, tiled=True),
-        lax.all_gather(share_down, "ctx", axis=1, tiled=True),
+        gather_around(share_down, "ctx", 1),
         lax.all_gather(share_small, "ctx", axis=1, tiled=True),
         lax.all_gather(share_jbias, "ctx", axis=1, tiled=True),
         lax.all_gather(share_upbias, "ctx", axis=0, tiled=True),

time: 1360 us -> 1320 us (0.971)
  waiting for transfers between devices: 942 us -> 854 us
  local copies, waits for them, and re-layouts: 54.5 us -> 87.3 us
    all_gather x1 -> x0, waiting for transfers between devices: 46.1 us -> none  [local(): lax.all_gather(share_down, 'ctx', axis=1, tiled=True)]
    unnamed x19 -> x18, waiting for transfers between devices: 130 us -> 99.9 us
    dynamic_update_slice x0 -> x4, local copies, waits for them, and re-layouts: none -> 24.8 us  [gather_around(): lax.dynamic_update_slice_in_dim(filled, current, holder * extent, axis=dim)]
    ppermute x0 -> x3, waiting for transfers between devices: none -> 15.5 us  [gather_around(): current = lax.ppermute(current, axis, right)]
    psum x1, waiting for transfers between devices: 33.3 us -> 17.9 us  [local(): mixed_all = lax.psum(partial_value, 'tp')]
  transfers between devices with their start and end apart: 17 -> 19, of which waited for: 16 -> 16; matrix products, arithmetic and copies ran while one was open for 19% -> 22% of each run, Pallas kernels for 0% -> 0%
where the time goes in v1:
time: 1320 us; the launch traced here: 1310 us
  waiting for transfers between devices  854 us (65%)
  matrix products  161 us (12%)
  blocking collectives  138 us (10%)
  local copies, waits for them, and re-layouts  87.3 us (7%)
  other arithmetic  52.6 us (4%)
  between operations  15.5 us (1%)
    reduce_scatter x1, waiting for transfers between devices, local(): lax.psum_scatter(grad_down_w, ('fsdp', 'ctx'), scatter_dimension=1, tiled...  182 us
    reduce_scatter x1, waiting for transfers between devices, local(): lax.psum_scatter(grad_up_w, ('fsdp', 'ctx'), scatter_dimension=0, tiled=T...  150 us
    reduce_scatter x1, waiting for transfers between devices, local(): lax.psum_scatter(grad_joint_w, ('fsdp', 'ctx'), scatter_dimension=0, tile...  137 us
    unnamed x18, waiting for transfers between devices  99.9 us
    reduce_scatter x1, waiting for transfers between devices, local(): lax.psum_scatter(jnp.concatenate([key_part.reshape(count_rows * lax.axis_...  95 us
    unnamed x1, blocking collectives  50.5 us
    all_gather x1, waiting for transfers between devices, local(): lax.all_gather(keys_here, 'ctx', axis=0, tiled=True)  44.2 us
    all_gather x1, waiting for transfers between devices, local(): lax.all_gather(share_up, 'ctx', axis=0, tiled=True)  30.2 us
  transfers between devices with their start and end apart: 19, of which 16 were waited for; matrix products, arithmetic and copies ran while one was open for 22% of the time, Pallas kernels for 0%

profile of v1, /device:TPU:0, one launch (start us, length us, event | category | flops | bytes accessed | tf_op | source)
XLA Modules:
  0.0 1309.6 jit_solution(13507901342852622025)
XLA Ops:
  31.2 26.0 %all-gather.14.cloned.1.call-done = bf16[1024,3,512]{0,2,1:T(8,128)(2,1)} async-done(((bf16[256,3,512]{0,2,1:T(8,128)(2,1)}), bf16[1024,3,512]{0,2,1:T(8,128)(2,1)}) %all-gather.14.cloned.1.call-update) | async-done | bytes 3145744 | tf_op jit(solution)/shard_map/all_gather | solution.py:110
  67.5 11.9 all-gather
  89.5 44.2 %all-gather.18.cloned.1.call-done = bf16[2048,8,64]{0,2,1:T(8,128)(2,1)} async-done(((bf16[512,8,64]{0,2,1:T(8,128)(2,1)}), bf16[2048,8,64]{0,2,1:T(8,128)(2,1)}) %all-gather.18.cloned.1.call-update) | async-done | bytes 2097168 | tf_op jit(solution)/shard_map/all_gather | solution.py:140
  133.6 16.0 %fusion = (f32[8,512]{1,0:T(8,128)S(1)}, f32[8,512,2048]{2,1,0:T(8,128)}) fusion(pred[512,2048]{1,0:T(8,128)(4,1)S(1)} %fusion.7, bf16[2048,8,64]{0,2,1:T(8,128)(2,1)} %all-gather.18.cloned.1.call-done, bf16[512,8,48]{0,2,1:T(8,128)(2,1)S(1)} %slice.170, bf16[512,8,8]{0,2,1:T(8,128)(2,1)} %get-tuple-element.148, bf16[512,8,8]{0,2,1:T(8,128)(2,1)} %get-tuple-element.147), kind=kOutput, calls=%fused_computation.4 | convolution fusion | flops 1100476416 | bytes 37240832 | tf_op jit(solution)/shard_map/while/body/eval_jaxpr/qhe,khe->hqk/dot_general | solution.py:68
  149.6 15.9 %exponential_reduce_fusion = f32[8,512]{1,0:T(8,128)S(1)} fusion(f32[8,512,2048]{2,1,0:T(8,128)} %get-tuple-element.176, f32[8,512]{1,0:T(8,128)S(1)} %get-tuple-element.175, pred[512,2048]{1,0:T(8,128)(4,1)S(1)} %fusion.7), kind=kLoop, calls=%fused_computation.2 | loop fusion | flops 33550336 | bytes 34635776 | tf_op jit(solution)/shard_map/while/body/eval_jaxpr/reduce_sum | solution.py:157
  180.3 12.4 multiply_reduce_fusion.2
  192.7 25.3 %multiply_convert_fusion = bf16[8,512,2048]{2,1,0:T(8,128)(2,1)} fusion(bf16[8,512,2048]{2,1,0:T(8,128)(2,1)} %exponential_convert_fusion, bf16[512,8,64]{0,2,1:T(8,128)(2,1)S(1)} %bitcast.212, bf16[2048,8,64]{0,2,1:T(8,128)(2,1)} %all-gather.16.cloned.1.call-done, f32[8,512]{1,0:T(8,128)S(1)} %bitcast.227), kind=kOutput, calls=%fused_computation | convolution fusion | flops 1107296256 | bytes 36192256 | tf_op jit(solution)/shard_map/while/body/eval_jaxpr/qhe,khe->hqk/dot_general | solution.py:202
  267.5 15.1 %multiply_convert_fusion.1 = (bf16[512,2048]{1,0:T(8,128)(2,1)}, f32[512,2048]{1,0:T(8,128)}, f32[512,2048]{1,0:T(8,128)}) fusion(f32[2048]{0:T(1024)S(1)} %bitcast.253, bf16[1024,2048]{1,0:T(8,128)(2,1)} %all-gather.22.cloned.1.call-done, bf16[1,512,1024]{2,1,0:T(8,128)(2,1)S(1)} %copy-done.3, f32[1024]{0:T(1024)S(1)} %bitcast.257, f32[1024]{0:T(1024)S(1)} %bitcast.234, ...), kind=kOutput, calls=%fused_computation.9 | convolution fusion | flops 2219835392 | bytes 15749120 | tf_op jit(solution)/shard_map/dot_general | solution.py:165
  320.6 12.7 fusion.41
  339.6 95.0 %reduce-scatter.12.cloned.1.call-done = f32[512,1024]{1,0:T(8,128)} async-done(((f32[2048,1024]{1,0:T(8,128)}), f32[512,1024]{1,0:T(8,128)}) %reduce-scatter.12.cloned.1.call-update) | async-done | bytes 2097168 | tf_op jit(solution)/shard_map/reduce_scatter | solution.py:227
  470.1 149.9 %reduce-scatter.18.cloned.1.call-done = f32[64,2048]{1,0:T(8,128)} async-done(((f32[1024,2048]{1,0:T(8,128)}), f32[64,2048]{1,0:T(8,128)}) %reduce-scatter.18.cloned.1.call-update) | async-done | bytes 524304 | tf_op jit(solution)/shard_map/reduce_scatter | solution.py:271
  620.1 182.1 %reduce-scatter.20.cloned.1.call-done = f32[2048,64]{0,1:T(8,128)} async-done(((f32[2048,1024]{0,1:T(8,128)}), f32[2048,64]{0,1:T(8,128)}) %reduce-scatter.20.cloned.1.call-update) | async-done | bytes 524304 | tf_op jit(solution)/shard_map/reduce_scatter | solution.py:272
  802.3 15.5 %collective-permute-done = f32[2048,64]{0,1:T(8,128)} collective-permute-done((f32[2048,64]{0,1:T(8,128)}, f32[2048,64]{0,1:T(8,128)}, u32[]{:S(2)}, u32[]{:S(2)}) %collective-permute-start) | collective-permute-done | bytes 524320 | tf_op jit(solution)/shard_map/ppermute | solution.py:21
  817.8 17.9 %all-reduce.4.cloned.1.call-done = (f32[512,1024]{1,0:T(8,128)}, f32[512,1024]{1,0:T(8,128)}, f32[512,1024]{1,0:T(8,128)}) async-done(((f32[512,1024]{1,0:T(8,128)}, f32[512,1024]{1,0:T(8,128)}, f32[512,1024]{1,0:T(8,128)}), (f32[512,1024]{1,0:T(8,128)}, f32[512,1024]{1,0:T(8,128)}, f32[512,1024]{1,0:T(8,128)})) %all-reduce.4.cloned.1.call-update) | async-done | bytes 6291472 | tf_op jit(solution)/shard_map/psum | solution.py:170
  840.2 137.3 %reduce-scatter.14.cloned.1.call-done = f32[64,3,512]{2,0,1:T(8,128)} async-done(((f32[1024,3,512]{2,0,1:T(8,128)}), f32[64,3,512]{2,0,1:T(8,128)}) %reduce-scatter.14.cloned.1.call-update) | async-done | bytes 393232 | tf_op jit(solution)/shard_map/reduce_scatter | solution.py:269
  978.9 50.5 %all-reduce = f32[2048]{0:T(1024)S(1)} all-reduce(f32[2048]{0:T(1024)S(1)} %get-tuple-element.179), channel_id=9, replica_groups=mesh['fsdp'=4,'ctx'=4,'tp'=2] {'fsdp','ctx'}, use_global_device_ids=true, to_apply=%region_25.26.clone | all-reduce | flops 2048 | bytes 16384
  1037.7 25.4 %reduce-scatter.16.cloned.1.call-done = f32[512,64]{0,1:T(8,128)} async-done(((f32[512,1024]{0,1:T(8,128)}), f32[512,64]{0,1:T(8,128)}) %reduce-scatter.16.cloned.1.call-update) | async-done | bytes 131088 | tf_op jit(solution)/shard_map/reduce_scatter | solution.py:270
  1063.1 15.9 %all_gather.65 = f32[512,256]{0,1:T(8,128)} all-gather(f32[512,64]{0,1:T(8,128)} %reduce-scatter.16.cloned.1.call-done), channel_id=1, replica_groups=mesh['fsdp'=4,'ctx'=4,'tp'=2] {'ctx'}, dimensions={1}, use_global_device_ids=true | all-gather | bytes 655360 | tf_op jit(solution)/shard_map/all_gather | solution.py:279
  1116.7 24.4 %reduce-scatter.24.cloned.1.call-done = f32[32,3]{1,0:T(8,128)} async-done(((f32[512,3]{1,0:T(8,128)}), f32[32,3]{1,0:T(8,128)}) %reduce-scatter.24.cloned.1.call-update) | async-done | bytes 400
  1141.9 12.1 all-gather.3
  1154.7 30.2 %all-gather.28.cloned.1.call-done = f32[256,2048]{1,0:T(8,128)} async-done(((f32[64,2048]{1,0:T(8,128)}), f32[256,2048]{1,0:T(8,128)}) %all-gather.28.cloned.1.call-update) | async-done | bytes 2097168 | tf_op jit(solution)/shard_map/all_gather | solution.py:280
  1189.8 73.5 %reduce-scatter.22.cloned.1.call-done = f32[64,6]{1,0:T(8,128)} async-done(((f32[1024,6]{1,0:T(8,128)}), f32[64,6]{1,0:T(8,128)}) %reduce-scatter.22.cloned.1.call-update) | async-done | bytes 1552
  1264.1 13.4 %all-gather.2 = f32[4,64,6]{1,2,0:T(8,128)S(1)} all-gather(f32[1,64,6]{1,2,0:T(8,128)S(1)} %bitcast.243), channel_id=1, replica_groups=mesh['fsdp'=4,'ctx'=4,'tp'=2] {'ctx'}, dimensions={0}, use_global_device_ids=true | all-gather | bytes 7680 | tf_op jit(solution)/shard_map/all_gather | solution.py:282
  1278.2 20.2 %all-gather.26.cloned.1.call-done = f32[256,3,512]{2,0,1:T(8,128)} async-done(((f32[64,3,512]{2,0,1:T(8,128)}), f32[256,3,512]{2,0,1:T(8,128)}) %all-gather.26.cloned.1.call-update) | async-done | bytes 1572880 | tf_op jit(solution)/shard_map/all_gather | solution.py:278
  (201 shorter events, 251.6 us)
Async XLA Ops:
  7.3 49.9 %all-gather.14.cloned.1.call-start = ((), (), s32[]{:S(2)}) async-start(), calls=%async_computation.7 | async-start | bytes 3932160 | tf_op jit(solution)/shard_map/all_gather | solution.py:110
  9.7 75.8 %all-gather.20.cloned.1.call-start = ((), (), s32[]{:S(2)}) async-start(), calls=%async_computation.10 | async-start | bytes 1310720 | tf_op jit(solution)/shard_map/all_gather | solution.py:111
  10.5 123.2 %all-gather.18.cloned.1.call-start = ((), (), s32[]{:S(2)}) async-start(), calls=%async_computation.9 | async-start | bytes 2621440 | tf_op jit(solution)/shard_map/all_gather | solution.py:140
  64.1 116.3 %all-gather.16.cloned.1.call-start = ((), (), s32[]{:S(2)}) async-start(), calls=%async_computation.8 | async-start | bytes 2621440 | tf_op jit(solution)/shard_map/all_gather | solution.py:141
  66.2 201.3 %all-gather.22.cloned.1.call-start = ((), (), s32[]{:S(2)}) async-start(), calls=%async_computation.11 | async-start | bytes 5242880 | tf_op jit(solution)/shard_map/all_gather | solution.py:112
  66.8 221.0 %all-gather.24.cloned.1.call-start = ((), (), s32[]{:S(2)}) async-start(), calls=%async_computation.12 | async-start | bytes 5242880 | tf_op jit(solution)/shard_map/all_gather | solution.py:113
  67.4 367.3 %reduce-scatter.12.cloned.1.call-start = ((), (), s32[]{:S(2)}) async-start(), calls=%async_computation.13 | async-start | bytes 10485760 | tf_op jit(solution)/shard_map/reduce_scatter | solution.py:227
  258.8 361.2 %reduce-scatter.18.cloned.1.call-start = ((), (), s32[]{:S(2)}) async-start(), calls=%async_computation.17 | async-start | bytes 8912896 | tf_op jit(solution)/shard_map/reduce_scatter | solution.py:271
  302.5 499.7 %reduce-scatter.20.cloned.1.call-start = ((), (), s32[]{:S(2)}) async-start(), calls=%async_computation.19 | async-start | bytes 8912896 | tf_op jit(solution)/shard_map/reduce_scatter | solution.py:272
  309.8 525.9 %all-reduce.4.cloned.1.call-start = ((), (), s32[]{:S(2)}) async-start(), calls=%async_computation.22 | async-start | bytes 12582912 | tf_op jit(solution)/shard_map/psum | solution.py:170
  339.6 101.8 %copy-start.11 = (f32[512,8]{0,1:T(8,128)S(1)}, f32[512,8]{0,1:T(8,128)}, u32[]{:S(2)}) copy-start(f32[512,8]{0,1:T(8,128)} %copy-done.10) | copy-start | bytes 49156
  339.6 101.8 %copy-start.13 = (f32[512,8]{0,1:T(8,128)S(1)}, f32[512,8]{0,1:T(8,128)}, u32[]{:S(2)}) copy-start(f32[512,8]{0,1:T(8,128)} %copy-done.12) | copy-start | bytes 49156
  456.6 521.0 %reduce-scatter.14.cloned.1.call-start = ((), (), s32[]{:S(2)}) async-start(), calls=%async_computation.14 | async-start | bytes 6684672 | tf_op jit(solution)/shard_map/reduce_scatter | solution.py:269
  463.8 599.3 %reduce-scatter.16.cloned.1.call-start = ((), (), s32[]{:S(2)}) async-start(), calls=%async_computation.16 | async-start | bytes 2228224 | tf_op jit(solution)/shard_map/reduce_scatter | solution.py:270
  467.0 674.1 %reduce-scatter.24.cloned.1.call-start = ((), (), s32[]{:S(2)}) async-start(), calls=%async_computation.21 | async-start | bytes 278528
  470.0 714.9 %all-gather.28.cloned.1.call-start = ((), (), s32[]{:S(2)}) async-start(), calls=%async_computation.18 | async-start | bytes 2621440 | tf_op jit(solution)/shard_map/all_gather | solution.py:280
  620.0 357.7 %copy-start.31 = (u32[32]{0:T(128)S(1)}, u32[32]{0:T(128)}, u32[]{:S(2)}) copy-start(u32[32]{0:T(128)} %constant.180) | copy-start | bytes 388
  620.0 643.3 %reduce-scatter.22.cloned.1.call-start = ((), (), s32[]{:S(2)}) async-start(), calls=%async_computation.20 | async-start | bytes 557056
  802.1 15.6 %collective-permute-start = (f32[2048,64]{0,1:T(8,128)}, f32[2048,64]{0,1:T(8,128)}, u32[]{:S(2)}, u32[]{:S(2)}) collective-permute-start(f32[2048,64]{0,1:T(8,128)} %reduce-scatter.20.cloned.1.call-done), channel_id=1, source_target_pairs={{0,2},{2,4},{4,6},{6,0},{1,3},{3,5},{5,7},{7,1},{8,10},{10,12},{12... | collective-permute-start | bytes 1572872 | tf_op jit(solution)/shard_map/ppermute | solution.py:21
  817.8 159.8 %collective-permute-start.1 = (f32[2048,64]{0,1:T(8,128)}, f32[2048,64]{0,1:T(8,128)}, u32[]{:S(2)}, u32[]{:S(2)}) collective-permute-start(f32[2048,64]{0,1:T(8,128)} %collective-permute-done), channel_id=1, source_target_pairs={{0,2},{2,4},{4,6},{6,0},{1,3},{3,5},{5,7},{7,1},{8,10},{10,12},{12... | collective-permute-start | bytes 1572872 | tf_op jit(solution)/shard_map/ppermute | solution.py:21
  840.2 458.2 %all-gather.26.cloned.1.call-start = ((), (), s32[]{:S(2)}) async-start(), calls=%async_computation.15 | async-start | bytes 1966080 | tf_op jit(solution)/shard_map/all_gather | solution.py:278
  977.5 129.9 %collective-permute-start.2 = (f32[2048,64]{0,1:T(8,128)}, f32[2048,64]{0,1:T(8,128)}, u32[]{:S(2)}, u32[]{:S(2)}) collective-permute-start(f32[2048,64]{0,1:T(8,128)} %collective-permute-done.1), channel_id=1, source_target_pairs={{0,2},{2,4},{4,6},{6,0},{1,3},{3,5},{5,7},{7,1},{8,10},{10,12},{12... | collective-permute-start | bytes 1572872 | tf_op jit(solution)/shard_map/ppermute | solution.py:21
  1099.6 85.4 %copy-start.17 = (f32[1,1024]{1,0:T(1,128)S(1)}, f32[1,1024]{1,0:T(1,128)}, u32[]{:S(2)}) copy-start(f32[1,1024]{1,0:T(1,128)} %get-tuple-element.160) | copy-start | bytes 12292
  1189.8 111.2 %copy-start.7 = (f32[256,2048]{1,0:T(8,128)S(1)}, f32[256,2048]{1,0:T(8,128)}, u32[]{:S(2)}) copy-start(f32[256,2048]{1,0:T(8,128)} %all-gather.28.cloned.1.call-done) | copy-start | bytes 6291460
  (29 other events, 434.1 us)
Sparse Core Ops, SparseCore 0:
  10.5 46.6 all-gather.13
  59.0 26.4 all-gather.19
  87.7 45.9 all-gather.17
  135.6 44.6 all-gather.15
  182.0 51.4 all-gather.21
  235.2 52.6 all-gather.23
  290.2 144.4 reduce-scatter.11
  436.9 183.0 reduce-scatter.17
  622.3 179.8 reduce-scatter.19
  805.9 29.7 all-reduce.3
  838.1 139.3 reduce-scatter.13
  980.3 82.7 reduce-scatter.15
  1065.4 75.6 reduce-scatter.23
  1142.6 42.3 all-gather.27
  1187.6 75.6 reduce-scatter.21
  1264.8 33.4 all-gather.25
